TPU v7x, 32 devices: a whole 2x2x4 slice. The times are simulated.
32 devices in a mesh: seq: 16 (over z, y, x), tp: 2 (over core).
Axes of the slice: x: 2, y: 2, z: 4, core: 2. Of those that a mesh axis runs over, the one named last changes fastest.
Arguments:
- tokens: bfloat16 [2048, 2048], P('seq'), may hold values from -6 to 6
- attn_gain: float32 [2048], replicated, may hold values from 0.1 to 1.9
- mlp_gain: float32 [2048], replicated, may hold values from 0.1 to 1.9
- w_query: float32 [2048, 2048], P('seq', 'tp'), may hold values from -0.70710678 to 0.70710678
- w_key: float32 [2048, 2048], P('seq', 'tp'), may hold values from -0.70710678 to 0.70710678
- w_value: float32 [2048, 2048], P('seq', 'tp'), may hold values from -0.125 to 0.125
- w_out: float32 [2048, 2048], P('tp', 'seq'), may hold values from -0.125 to 0.125
- sink_logits: float32 [16], P('tp'), may hold values from 8 to 16
- router: float32 [2048, 16], P('seq'), may hold values from -0.25 to 0.25
- expert_gate: float32 [16, 2048, 1024], P(None, 'seq', 'tp'), may hold values from -0.125 to 0.125
- expert_up: float32 [16, 2048, 1024], P(None, 'seq', 'tp'), may hold values from -0.125 to 0.125
- expert_down: float32 [16, 2048, 1024], P(None, 'seq', 'tp'), may hold values from -0.1875 to 0.1875
- layout_map: int32 [16], replicated, may hold values from 0 to 15, each once
- real_lengths: int32 [2], replicated, may hold values from 256 to 1088, as said below
- routes: int32 [2048, 8], P('seq'), may hold values from 0 to 15, all different within a row; in each aligned block of 128 rows (0 to 127, 128 to 255, ...) at most 72 rows name the same one
Outputs:
- layer_out: bfloat16 [2048, 2048], P('seq', 'tp')
Inputs may be any that keep to these rules, and one draw needn't show every extreme that they name: Prompt p has real tokens in the first real_lengths[p] of its slots and padding after them; each length is at least 256; the last prompt has no padding. `routes`: each row names 8 different experts; among the rows of one device no expert is named more than 72 times, and in some device some expert exactly 72 times. `layout_map`: each trainer expert is held by exactly one server expert number.
All inputs are finite; a program needn't handle non-finite values.
Results may differ from a plain program's by a relative error of at most 0.0075.
The roundings to bfloat16 on the way count: a program that leaves them out, or rounds other values in their place, can miss the bound.
Values may be sent and summed in bfloat16 or wider, within the bound.
No kernel may reach another device: no remote copies, remote signals or barrier semaphores. Data moves between devices by JAX's collectives and lax.ppermute only.
A program may use at most 128 MiB of HBM per device.

v0:
```python
import jax
import jax.numpy as jnp
from jax import lax
from jax.sharding import PartitionSpec as P

HEAD = 128
HALF_WIN = 2048
EPSILON = 1e-05
ROPE_BASE = 50000.0
MASKED = -1e30


def from_behind(value, axis, steps):
    count = lax.axis_size(axis)
    first, last = (max(0, -steps), min(count, count - steps))
    return lax.ppermute(value, axis, [(source, source + steps) for source in range(first, last)])


def rms_scale(row_values, gain_vector):
    mean_square = jnp.mean(row_values * row_values, axis=-1, keepdims=True)
    return row_values * lax.rsqrt(mean_square + EPSILON) * gain_vector


def rotate(head_block, positions):
    half_dim = head_block.shape[-1] // 2
    frequency = ROPE_BASE ** (-jnp.arange(half_dim, dtype=jnp.float32) / half_dim)
    angles = positions[:, None, None] * frequency[None, None, :]
    cosine = jnp.cos(angles)
    sine_part = jnp.sin(angles)
    first_half = head_block[..., :half_dim]
    second_half = head_block[..., half_dim:]
    return jnp.concatenate(
        [
            first_half * cosine - second_half * sine_part,
            second_half * cosine + first_half * sine_part,
        ],
        axis=-1,
    )


def length_of(prompt, real_lengths):
    one_hot = prompt[:, None] == jnp.arange(real_lengths.shape[0], dtype=jnp.int32)[None, :]
    return jnp.sum(jnp.where(one_hot, real_lengths[None, :], 0), axis=1)


def prompt_split(slot_ids, slot_len, stagger, prompt_count):
    prompt = jnp.minimum((slot_ids + stagger) // slot_len, prompt_count - 1)
    start = jnp.maximum(prompt * slot_len - stagger, 0)
    return (prompt, slot_ids - start)


def key_rules(query_ids, key_ids, slot_len, stagger, total_slots, real_lengths):
    prompt_count = real_lengths.shape[0]
    key_prompt, key_pos = prompt_split(key_ids, slot_len, stagger, prompt_count)
    query_prompt = prompt_split(query_ids, slot_len, stagger, prompt_count)[0]
    inside = (key_ids >= 0) & (key_ids < total_slots)
    key_live = inside & (key_pos < length_of(key_prompt, real_lengths))
    same_prompt = query_prompt[:, None] == key_prompt[None, :]
    nearby = jnp.abs(query_ids[:, None] - key_ids[None, :]) < HALF_WIN
    return same_prompt & nearby & key_live[None, :]


def attend(softmax_state, query_rows, key_rows, value_rows, allowed):
    running_max, denominator, accumulated = softmax_state
    scores = jnp.einsum(
        "tge,kge->gtk", query_rows, key_rows, preferred_element_type=jnp.float32
    ) * HEAD ** (-0.5)
    scores = jnp.where(allowed[None], scores, MASKED)
    new_max = jnp.maximum(running_max, jnp.max(scores, axis=2))
    rescale = jnp.exp(running_max - new_max)
    weight_tensors = jnp.exp(scores - new_max[:, :, None])
    denominator = denominator * rescale + jnp.sum(weight_tensors, axis=2)
    accumulated = accumulated * rescale[:, :, None] + jnp.einsum(
        "ytz,zyb->ytb",
        weight_tensors,
        value_rows.astype(jnp.float32),
        precision=lax.Precision.HIGHEST,
    )
    return (new_max, denominator, accumulated)


def shards(
    tokens,
    attn_gain,
    mlp_gain,
    w_query,
    w_key,
    w_value,
    w_out,
    sink_logits,
    router,
    expert_gate,
    expert_up,
    expert_down,
    layout_map,
    real_lengths,
    routes,
):
    token_count, model_width = tokens.shape
    seq_count = lax.axis_size("seq")
    tp_count = lax.axis_size("tp")
    expert_count = router.shape[1]
    route_count = routes.shape[1]
    head_count = sink_logits.shape[0]
    proj_width = head_count * HEAD
    col_share = model_width // tp_count
    total_slots = token_count * seq_count
    prompt_count = real_lengths.shape[0]
    slot_len = total_slots // prompt_count
    stagger = token_count // 2
    capacity = max(2, min(token_count, 9 * token_count * route_count // (8 * expert_count)))
    seq_place = lax.axis_index("seq")
    tp_place = lax.axis_index("tp")
    offsets = jnp.arange(token_count, dtype=jnp.int32)
    token_index = seq_place * token_count + offsets
    prompt, position = prompt_split(token_index, slot_len, stagger, prompt_count)
    valid_token = position < length_of(prompt, real_lengths)
    normed = rms_scale(tokens.astype(jnp.float32), attn_gain).astype(jnp.bfloat16)
    stack_local = jnp.concatenate([w_query, w_key, w_value], axis=1).astype(jnp.bfloat16)
    router_local = router.astype(jnp.bfloat16)
    stack_piece = lax.all_gather(stack_local, "seq", axis=0, tiled=True)
    router_piece = lax.all_gather(router_local, "seq", axis=0, tiled=True)
    product = jnp.dot(normed, stack_piece, preferred_element_type=jnp.float32)
    router_full = router_piece
    product, router_full = (product, router_full)
    rotary_positions = position.astype(jnp.float32)
    query_rows = rotate(
        product[:, :proj_width].reshape(token_count, head_count, HEAD), rotary_positions
    ).astype(jnp.bfloat16)
    key_rows = rotate(
        product[:, proj_width : 2 * proj_width].reshape(token_count, head_count, HEAD),
        rotary_positions,
    ).astype(jnp.bfloat16)
    value_rows = (
        product[:, 2 * proj_width :].astype(jnp.bfloat16).reshape(token_count, head_count, HEAD)
    )
    softmax_state = (
        jnp.broadcast_to(sink_logits[:, None], (head_count, token_count)),
        jnp.ones((head_count, token_count), jnp.float32),
        jnp.zeros((head_count, token_count, HEAD), jnp.float32),
    )
    softmax_state = attend(
        softmax_state,
        query_rows,
        key_rows,
        value_rows,
        key_rules(token_index, token_index, slot_len, stagger, total_slots, real_lengths),
    )
    own_pair = jnp.stack([key_rows, value_rows])

    def one_turn(turn_index, loop_carry):
        loop_state, from_below, from_above = loop_carry
        from_below = from_behind(from_below, "seq", 1)
        from_above = from_behind(from_above, "seq", -1)
        reach_rows = (turn_index + 1) * token_count
        key_ids = jnp.concatenate([token_index - reach_rows, token_index + reach_rows])
        neighbours = jnp.concatenate([from_below, from_above], axis=1)
        allowed = key_rules(token_index, key_ids, slot_len, stagger, total_slots, real_lengths)
        loop_state = attend(loop_state, query_rows, neighbours[0], neighbours[1], allowed)
        return (loop_state, from_below, from_above)

    softmax_state, from_below, from_above = lax.fori_loop(
        0, HALF_WIN // token_count, one_turn, (softmax_state, own_pair, own_pair)
    )
    running_max, denominator, accumulated = softmax_state
    attention_result = (
        jnp.transpose(accumulated / denominator[:, :, None], (1, 0, 2))
        .reshape(token_count, proj_width)
        .astype(jnp.bfloat16)
    )
    partial_out = jnp.dot(
        attention_result,
        lax.all_gather(w_out.astype(jnp.bfloat16), "seq", axis=1, tiled=True),
        preferred_element_type=jnp.float32,
    )
    mixed_full = lax.psum(partial_out, "tp")
    full_rows = tokens.astype(jnp.float32) + mixed_full
    outgoing = rms_scale(full_rows, mlp_gain).astype(jnp.bfloat16)
    logits = jnp.dot(outgoing, router_full, preferred_element_type=jnp.float32)
    residual = lax.dynamic_slice_in_dim(full_rows, tp_place * col_share, col_share, 1)
    expert_ids = jnp.arange(expert_count, dtype=jnp.int32)
    chosen = routes[:, :, None] == expert_ids[None, None, :]
    route_logits = jnp.sum(jnp.where(chosen, logits[:, None, :], 0.0), axis=2)
    route_weight = jax.nn.softmax(route_logits, axis=1) * valid_token[:, None]
    flat_routes = routes.reshape(-1)
    live_route = jnp.repeat(valid_token, route_count)
    one_hot = ((flat_routes[:, None] == expert_ids[None, :]) & live_route[:, None]).astype(
        jnp.int32
    )
    rank_within = jnp.sum((jnp.cumsum(one_hot, axis=0) - one_hot) * one_hot, axis=1)
    slot_index = flat_routes * capacity + rank_within
    target_slot = jnp.where(live_route, slot_index, expert_count * capacity)
    owner_row = jnp.repeat(offsets, route_count) + 1
    source_row = (
        jnp.zeros((expert_count * capacity,), jnp.int32).at[target_slot].set(owner_row, mode="drop")
    )
    buffer = jnp.where(
        (source_row > 0)[:, None],
        outgoing[jnp.maximum(source_row - 1, 0)],
        jnp.zeros((), jnp.bfloat16),
    )
    buffer = buffer.reshape(expert_count, capacity, outgoing.shape[1])
    trainer = jnp.concatenate([expert_gate, expert_up, expert_down], axis=2).astype(jnp.bfloat16)
    ordered = jnp.take(trainer, layout_map, axis=0)
    server = lax.all_to_all(ordered, "seq", split_axis=0, concat_axis=1, tiled=True)
    hidden_share = expert_gate.shape[2]
    local_experts = server.shape[0]
    full_block = lax.all_to_all(buffer, "seq", split_axis=0, concat_axis=0, tiled=True)
    item_count = full_block.shape[1]
    grouped = full_block.reshape(seq_count, local_experts, item_count, model_width)
    gate_up = jnp.einsum(
        "sacd,adf->sacf",
        grouped,
        server[:, :, : 2 * hidden_share],
        preferred_element_type=jnp.float32,
    )
    hidden_state = (jax.nn.silu(gate_up[..., :hidden_share]) * gate_up[..., hidden_share:]).astype(
        jnp.bfloat16
    )
    partial_rows = jnp.einsum(
        "sacf,adf->sacd",
        hidden_state,
        server[:, :, 2 * hidden_share :],
        preferred_element_type=jnp.float32,
    )
    partial_rows = lax.optimization_barrier(partial_rows.astype(jnp.bfloat16)).astype(jnp.float32)
    summed = lax.psum_scatter(
        partial_rows.astype(jnp.bfloat16), "tp", scatter_dimension=3, tiled=True
    )
    returned = lax.all_to_all(
        summed.reshape(seq_count * local_experts, item_count, col_share),
        "seq",
        split_axis=0,
        concat_axis=0,
        tiled=True,
    )
    picked = returned.reshape(expert_count * capacity, col_share)[
        jnp.where(live_route, slot_index, 0)
    ]
    picked = picked.reshape(token_count, route_count, col_share)
    expert_mix = jnp.sum(route_weight[:, :, None] * picked.astype(jnp.float32), axis=1)
    return (residual + expert_mix).astype(jnp.bfloat16)


def solution(mesh):
    placed = (
        P("seq", None),
        P(),
        P(),
        P("seq", "tp"),
        P("seq", "tp"),
        P("seq", "tp"),
        P("tp", "seq"),
        P("tp"),
        P("seq", None),
        P(None, "seq", "tp"),
        P(None, "seq", "tp"),
        P(None, "seq", "tp"),
        P(),
        P(),
        P("seq", None),
    )
    return jax.shard_map(
        shards, mesh=mesh, in_specs=placed, out_specs=P("seq", "tp"), check_vma=False
    )
```

profile of v0, /device:TPU:18, one launch (start us, length us, event | category | flops | bytes accessed | tf_op | source)
XLA Modules:
  0.0 1064.2 jit_solution(7470347210897196199)
XLA Ops:
  35.2 7.2 all-to-all-start
  50.4 233.6 %all-gather.3.cloned.1.call-done = bf16[2048,3072]{1,0:T(8,128)(2,1)} async-done(((bf16[128,3072]{1,0:T(8,128)(2,1)}), bf16[2048,3072]{1,0:T(8,128)(2,1)}) %all-gather.3.cloned.1.call-update) | async-done | bytes 12582928 | tf_op jit(solution)/shard_map/all_gather | solution.py:121
  293.4 493.8 %while.25 = (s32[]{:T(128)}, f32[8,128]{1,0:T(8,128)S(1)}, f32[8,128]{1,0:T(8,128)S(1)}, f32[8,128,128]{2,1,0:T(8,128)S(1)}, bf16[2,128,8,128]{3,1,2,0:T(8,128)(...) while((s32[]{:T(128)}, f32[8,128]{1,0:T(8,128)S(1)}, ...), condition=%wide.region_8.9_spmd.clone, body=%wide.region_4.8_spmd.clone.sunk | while | flops 471806848 | bytes 14038749 | solution.py:162
  300.5 23.3 %collective-permute-done = bf16[2,128,8,128]{3,1,2,0:T(8,128)(2,1)S(1)} collective-permute-done((bf16[2,128,8,128]{3,1,2,0:T(8,128)(2,1)S(1)}, bf16[2,128,8,128]{3,1,2,0:T(8,128)(2,1)S(1)}, u32[]{:S(2)}, u32[]{:S(2)}) %collective-permute-start) | collective-permute-done | bytes 524320 | tf_op jit(solution)/shard_map/while/body/eval_jaxpr/ppermute | solution.py:16
  332.8 20.7 %collective-permute-done = bf16[2,128,8,128]{3,1,2,0:T(8,128)(2,1)S(1)} collective-permute-done((bf16[2,128,8,128]{3,1,2,0:T(8,128)(2,1)S(1)}, bf16[2,128,8,128]{3,1,2,0:T(8,128)(2,1)S(1)}, u32[]{:S(2)}, u32[]{:S(2)}) %collective-permute-start) | collective-permute-done | bytes 524320 | tf_op jit(solution)/shard_map/while/body/eval_jaxpr/ppermute | solution.py:16
  362.5 41.4 %collective-permute-done = bf16[2,128,8,128]{3,1,2,0:T(8,128)(2,1)S(1)} collective-permute-done((bf16[2,128,8,128]{3,1,2,0:T(8,128)(2,1)S(1)}, bf16[2,128,8,128]{3,1,2,0:T(8,128)(2,1)S(1)}, u32[]{:S(2)}, u32[]{:S(2)}) %collective-permute-start) | collective-permute-done | bytes 524320 | tf_op jit(solution)/shard_map/while/body/eval_jaxpr/ppermute | solution.py:16
  413.3 21.1 %collective-permute-done = bf16[2,128,8,128]{3,1,2,0:T(8,128)(2,1)S(1)} collective-permute-done((bf16[2,128,8,128]{3,1,2,0:T(8,128)(2,1)S(1)}, bf16[2,128,8,128]{3,1,2,0:T(8,128)(2,1)S(1)}, u32[]{:S(2)}, u32[]{:S(2)}) %collective-permute-start) | collective-permute-done | bytes 524320 | tf_op jit(solution)/shard_map/while/body/eval_jaxpr/ppermute | solution.py:16
  443.4 19.8 %collective-permute-done = bf16[2,128,8,128]{3,1,2,0:T(8,128)(2,1)S(1)} collective-permute-done((bf16[2,128,8,128]{3,1,2,0:T(8,128)(2,1)S(1)}, bf16[2,128,8,128]{3,1,2,0:T(8,128)(2,1)S(1)}, u32[]{:S(2)}, u32[]{:S(2)}) %collective-permute-start) | collective-permute-done | bytes 524320 | tf_op jit(solution)/shard_map/while/body/eval_jaxpr/ppermute | solution.py:16
  472.2 19.4 %collective-permute-done = bf16[2,128,8,128]{3,1,2,0:T(8,128)(2,1)S(1)} collective-permute-done((bf16[2,128,8,128]{3,1,2,0:T(8,128)(2,1)S(1)}, bf16[2,128,8,128]{3,1,2,0:T(8,128)(2,1)S(1)}, u32[]{:S(2)}, u32[]{:S(2)}) %collective-permute-start) | collective-permute-done | bytes 524320 | tf_op jit(solution)/shard_map/while/body/eval_jaxpr/ppermute | solution.py:16
  500.7 21.3 %collective-permute-done = bf16[2,128,8,128]{3,1,2,0:T(8,128)(2,1)S(1)} collective-permute-done((bf16[2,128,8,128]{3,1,2,0:T(8,128)(2,1)S(1)}, bf16[2,128,8,128]{3,1,2,0:T(8,128)(2,1)S(1)}, u32[]{:S(2)}, u32[]{:S(2)}) %collective-permute-start) | collective-permute-done | bytes 524320 | tf_op jit(solution)/shard_map/while/body/eval_jaxpr/ppermute | solution.py:16
  531.0 19.4 %collective-permute-done = bf16[2,128,8,128]{3,1,2,0:T(8,128)(2,1)S(1)} collective-permute-done((bf16[2,128,8,128]{3,1,2,0:T(8,128)(2,1)S(1)}, bf16[2,128,8,128]{3,1,2,0:T(8,128)(2,1)S(1)}, u32[]{:S(2)}, u32[]{:S(2)}) %collective-permute-start) | collective-permute-done | bytes 524320 | tf_op jit(solution)/shard_map/while/body/eval_jaxpr/ppermute | solution.py:16
  559.4 21.3 %collective-permute-done = bf16[2,128,8,128]{3,1,2,0:T(8,128)(2,1)S(1)} collective-permute-done((bf16[2,128,8,128]{3,1,2,0:T(8,128)(2,1)S(1)}, bf16[2,128,8,128]{3,1,2,0:T(8,128)(2,1)S(1)}, u32[]{:S(2)}, u32[]{:S(2)}) %collective-permute-start) | collective-permute-done | bytes 524320 | tf_op jit(solution)/shard_map/while/body/eval_jaxpr/ppermute | solution.py:16
  589.7 19.4 %collective-permute-done = bf16[2,128,8,128]{3,1,2,0:T(8,128)(2,1)S(1)} collective-permute-done((bf16[2,128,8,128]{3,1,2,0:T(8,128)(2,1)S(1)}, bf16[2,128,8,128]{3,1,2,0:T(8,128)(2,1)S(1)}, u32[]{:S(2)}, u32[]{:S(2)}) %collective-permute-start) | collective-permute-done | bytes 524320 | tf_op jit(solution)/shard_map/while/body/eval_jaxpr/ppermute | solution.py:16
  618.1 21.3 %collective-permute-done = bf16[2,128,8,128]{3,1,2,0:T(8,128)(2,1)S(1)} collective-permute-done((bf16[2,128,8,128]{3,1,2,0:T(8,128)(2,1)S(1)}, bf16[2,128,8,128]{3,1,2,0:T(8,128)(2,1)S(1)}, u32[]{:S(2)}, u32[]{:S(2)}) %collective-permute-start) | collective-permute-done | bytes 524320 | tf_op jit(solution)/shard_map/while/body/eval_jaxpr/ppermute | solution.py:16
  648.4 19.4 %collective-permute-done = bf16[2,128,8,128]{3,1,2,0:T(8,128)(2,1)S(1)} collective-permute-done((bf16[2,128,8,128]{3,1,2,0:T(8,128)(2,1)S(1)}, bf16[2,128,8,128]{3,1,2,0:T(8,128)(2,1)S(1)}, u32[]{:S(2)}, u32[]{:S(2)}) %collective-permute-start) | collective-permute-done | bytes 524320 | tf_op jit(solution)/shard_map/while/body/eval_jaxpr/ppermute | solution.py:16
  676.9 21.3 %collective-permute-done = bf16[2,128,8,128]{3,1,2,0:T(8,128)(2,1)S(1)} collective-permute-done((bf16[2,128,8,128]{3,1,2,0:T(8,128)(2,1)S(1)}, bf16[2,128,8,128]{3,1,2,0:T(8,128)(2,1)S(1)}, u32[]{:S(2)}, u32[]{:S(2)}) %collective-permute-start) | collective-permute-done | bytes 524320 | tf_op jit(solution)/shard_map/while/body/eval_jaxpr/ppermute | solution.py:16
  707.2 19.4 %collective-permute-done = bf16[2,128,8,128]{3,1,2,0:T(8,128)(2,1)S(1)} collective-permute-done((bf16[2,128,8,128]{3,1,2,0:T(8,128)(2,1)S(1)}, bf16[2,128,8,128]{3,1,2,0:T(8,128)(2,1)S(1)}, u32[]{:S(2)}, u32[]{:S(2)}) %collective-permute-start) | collective-permute-done | bytes 524320 | tf_op jit(solution)/shard_map/while/body/eval_jaxpr/ppermute | solution.py:16
  735.6 21.3 %collective-permute-done = bf16[2,128,8,128]{3,1,2,0:T(8,128)(2,1)S(1)} collective-permute-done((bf16[2,128,8,128]{3,1,2,0:T(8,128)(2,1)S(1)}, bf16[2,128,8,128]{3,1,2,0:T(8,128)(2,1)S(1)}, u32[]{:S(2)}, u32[]{:S(2)}) %collective-permute-start) | collective-permute-done | bytes 524320 | tf_op jit(solution)/shard_map/while/body/eval_jaxpr/ppermute | solution.py:16
  765.9 19.4 %collective-permute-done = bf16[2,128,8,128]{3,1,2,0:T(8,128)(2,1)S(1)} collective-permute-done((bf16[2,128,8,128]{3,1,2,0:T(8,128)(2,1)S(1)}, bf16[2,128,8,128]{3,1,2,0:T(8,128)(2,1)S(1)}, u32[]{:S(2)}, u32[]{:S(2)}) %collective-permute-start) | collective-permute-done | bytes 524320 | tf_op jit(solution)/shard_map/while/body/eval_jaxpr/ppermute | solution.py:16
  796.2 15.8 %all-reduce.2.cloned.1.call-done = f32[128,2048]{1,0:T(8,128)} async-done(((f32[128,2048]{1,0:T(8,128)}), f32[128,2048]{1,0:T(8,128)}) %all-reduce.2.cloned.1.call-update) | async-done | bytes 1048592 | tf_op jit(solution)/shard_map/psum | solution.py:176
  825.4 110.3 %all_to_all.22 = bf16[16,72,2048]{2,1,0:T(8,128)(2,1)S(1)} all-to-all(bf16[16,72,2048]{2,1,0:T(8,128)(2,1)} %broadcast_select_fusion.1), channel_id=1, replica_groups=mesh['seq'=16,'tp'=2] {'seq'}, dimensions={0} | all-to-all | bytes 9437184 | tf_op jit(solution)/shard_map/all_to_all | solution.py:208
  935.7 7.3 fusion.14
  949.0 13.0 %reduce-scatter.2.cloned.1.call-done = bf16[16,1,72,1024]{3,2,0,1:T(8,128)(2,1)} async-done(((bf16[16,1,72,2048]{3,2,0,1:T(8,128)(2,1)}), bf16[16,1,72,1024]{3,2,0,1:T(8,128)(2,1)}) %reduce-scatter.2.cloned.1.call-update) | async-done | bytes 2359312 | tf_op jit(solution)/shard_map/reduce_scatter | solution.py:227
  968.9 78.2 %all_gather.11 = bf16[2048,16]{0,1:T(8,128)(2,1)S(1)} all-gather(bf16[128,16]{0,1:T(8,128)(2,1)S(1)} %convert_element_type.94), channel_id=1, replica_groups=mesh['seq'=16,'tp'=2] {'seq'}, dimensions={0}, use_global_device_ids=true | all-gather | bytes 69632 | tf_op jit(solution)/shard_map/all_gather | solution.py:122
  (431 shorter events, 233.7 us)
Async XLA Ops:
  6.5 277.4 %all-gather.3.cloned.1.call-start = ((), (), s32[]{:S(2)}) async-start(), calls=%async_computation.4 | async-start | bytes 13369344 | tf_op jit(solution)/shard_map/all_gather | solution.py:121
  35.2 790.3 %all-to-all-start = ((bf16[16,128,1536]{2,1,0:T(8,128)(2,1)}), bf16[16,128,1536]{2,1,0:T(8,128)(2,1)}, u32[]{:S(2)}, u32[]{:S(2)}) async-start(bf16[16,128,1536]{2,1,0:T(8,128)(2,1)} %broadcast_select_fusion), calls=%async_computation | async-start | bytes 12582912 | tf_op jit(solution)/shard_map/all_to_all | solution.py:205
  42.4 745.1 %all-gather.5.cloned.1.call-start = ((), (), s32[]{:S(2)}) async-start(), calls=%async_computation.5 | async-start | bytes 4456448 | tf_op jit(solution)/shard_map/all_gather | solution.py:173
  43.2 768.7 %all-reduce.2.cloned.1.call-start = ((), (), s32[]{:S(2)}) async-start(), calls=%async_computation.6 | async-start | bytes 2097152 | tf_op jit(solution)/shard_map/psum | solution.py:176
  293.4 30.4 %collective-permute-start.1 = (bf16[2,128,8,128]{3,1,2,0:T(8,128)(2,1)S(1)}, bf16[2,128,8,128]{3,1,2,0:T(8,128)(2,1)S(1)}, u32[]{:S(2)}, u32[]{:S(2)}) collective-permute-start(bf16[2,128,8,128]{3,1,2,0:T(8,128)(2,1)S(1)} %get-tuple-element.428), channel_id=1, source_target_pairs={{2,0},{4,2},{6,4},{8,6},{10,8},{12,10},{14,12},{16,14},{18,16},{20... | collective-permute-start | bytes 1572872 | tf_op jit(solution)/shard_map/while/body/eval_jaxpr/ppermute | solution.py:16
  296.1 27.7 %collective-permute-start = (bf16[2,128,8,128]{3,1,2,0:T(8,128)(2,1)S(1)}, bf16[2,128,8,128]{3,1,2,0:T(8,128)(2,1)S(1)}, u32[]{:S(2)}, u32[]{:S(2)}) collective-permute-start(bf16[2,128,8,128]{3,1,2,0:T(8,128)(2,1)S(1)} %get-tuple-element.427), channel_id=1, source_target_pairs={{0,2},{2,4},{4,6},{6,8},{8,10},{10,12},{12,14},{14,16},{16,18},{18... | collective-permute-start | bytes 1572872 | tf_op jit(solution)/shard_map/while/body/eval_jaxpr/ppermute | solution.py:16
  325.7 27.8 %collective-permute-start.1 = (bf16[2,128,8,128]{3,1,2,0:T(8,128)(2,1)S(1)}, bf16[2,128,8,128]{3,1,2,0:T(8,128)(2,1)S(1)}, u32[]{:S(2)}, u32[]{:S(2)}) collective-permute-start(bf16[2,128,8,128]{3,1,2,0:T(8,128)(2,1)S(1)} %get-tuple-element.428), channel_id=1, source_target_pairs={{2,0},{4,2},{6,4},{8,6},{10,8},{12,10},{14,12},{16,14},{18,16},{20... | collective-permute-start | bytes 1572872 | tf_op jit(solution)/shard_map/while/body/eval_jaxpr/ppermute | solution.py:16
  355.4 48.5 %collective-permute-start.1 = (bf16[2,128,8,128]{3,1,2,0:T(8,128)(2,1)S(1)}, bf16[2,128,8,128]{3,1,2,0:T(8,128)(2,1)S(1)}, u32[]{:S(2)}, u32[]{:S(2)}) collective-permute-start(bf16[2,128,8,128]{3,1,2,0:T(8,128)(2,1)S(1)} %get-tuple-element.428), channel_id=1, source_target_pairs={{2,0},{4,2},{6,4},{8,6},{10,8},{12,10},{14,12},{16,14},{18,16},{20... | collective-permute-start | bytes 1572872 | tf_op jit(solution)/shard_map/while/body/eval_jaxpr/ppermute | solution.py:16
  359.3 44.6 %collective-permute-start = (bf16[2,128,8,128]{3,1,2,0:T(8,128)(2,1)S(1)}, bf16[2,128,8,128]{3,1,2,0:T(8,128)(2,1)S(1)}, u32[]{:S(2)}, u32[]{:S(2)}) collective-permute-start(bf16[2,128,8,128]{3,1,2,0:T(8,128)(2,1)S(1)} %get-tuple-element.427), channel_id=1, source_target_pairs={{0,2},{2,4},{4,6},{6,8},{8,10},{10,12},{12,14},{14,16},{16,18},{18... | collective-permute-start | bytes 1572872 | tf_op jit(solution)/shard_map/while/body/eval_jaxpr/ppermute | solution.py:16
  405.8 28.7 %collective-permute-start.1 = (bf16[2,128,8,128]{3,1,2,0:T(8,128)(2,1)S(1)}, bf16[2,128,8,128]{3,1,2,0:T(8,128)(2,1)S(1)}, u32[]{:S(2)}, u32[]{:S(2)}) collective-permute-start(bf16[2,128,8,128]{3,1,2,0:T(8,128)(2,1)S(1)} %get-tuple-element.428), channel_id=1, source_target_pairs={{2,0},{4,2},{6,4},{8,6},{10,8},{12,10},{14,12},{16,14},{18,16},{20... | collective-permute-start | bytes 1572872 | tf_op jit(solution)/shard_map/while/body/eval_jaxpr/ppermute | solution.py:16
  407.7 26.7 %collective-permute-start = (bf16[2,128,8,128]{3,1,2,0:T(8,128)(2,1)S(1)}, bf16[2,128,8,128]{3,1,2,0:T(8,128)(2,1)S(1)}, u32[]{:S(2)}, u32[]{:S(2)}) collective-permute-start(bf16[2,128,8,128]{3,1,2,0:T(8,128)(2,1)S(1)} %get-tuple-element.427), channel_id=1, source_target_pairs={{0,2},{2,4},{4,6},{6,8},{8,10},{10,12},{12,14},{14,16},{16,18},{18... | collective-permute-start | bytes 1572872 | tf_op jit(solution)/shard_map/while/body/eval_jaxpr/ppermute | solution.py:16
  436.3 27.0 %collective-permute-start.1 = (bf16[2,128,8,128]{3,1,2,0:T(8,128)(2,1)S(1)}, bf16[2,128,8,128]{3,1,2,0:T(8,128)(2,1)S(1)}, u32[]{:S(2)}, u32[]{:S(2)}) collective-permute-start(bf16[2,128,8,128]{3,1,2,0:T(8,128)(2,1)S(1)} %get-tuple-element.428), channel_id=1, source_target_pairs={{2,0},{4,2},{6,4},{8,6},{10,8},{12,10},{14,12},{16,14},{18,16},{20... | collective-permute-start | bytes 1572872 | tf_op jit(solution)/shard_map/while/body/eval_jaxpr/ppermute | solution.py:16
  493.6 28.4 %collective-permute-start.1 = (bf16[2,128,8,128]{3,1,2,0:T(8,128)(2,1)S(1)}, bf16[2,128,8,128]{3,1,2,0:T(8,128)(2,1)S(1)}, u32[]{:S(2)}, u32[]{:S(2)}) collective-permute-start(bf16[2,128,8,128]{3,1,2,0:T(8,128)(2,1)S(1)} %get-tuple-element.428), channel_id=1, source_target_pairs={{2,0},{4,2},{6,4},{8,6},{10,8},{12,10},{14,12},{16,14},{18,16},{20... | collective-permute-start | bytes 1572872 | tf_op jit(solution)/shard_map/while/body/eval_jaxpr/ppermute | solution.py:16
  523.9 26.6 %collective-permute-start.1 = (bf16[2,128,8,128]{3,1,2,0:T(8,128)(2,1)S(1)}, bf16[2,128,8,128]{3,1,2,0:T(8,128)(2,1)S(1)}, u32[]{:S(2)}, u32[]{:S(2)}) collective-permute-start(bf16[2,128,8,128]{3,1,2,0:T(8,128)(2,1)S(1)} %get-tuple-element.428), channel_id=1, source_target_pairs={{2,0},{4,2},{6,4},{8,6},{10,8},{12,10},{14,12},{16,14},{18,16},{20... | collective-permute-start | bytes 1572872 | tf_op jit(solution)/shard_map/while/body/eval_jaxpr/ppermute | solution.py:16
  552.3 28.4 %collective-permute-start.1 = (bf16[2,128,8,128]{3,1,2,0:T(8,128)(2,1)S(1)}, bf16[2,128,8,128]{3,1,2,0:T(8,128)(2,1)S(1)}, u32[]{:S(2)}, u32[]{:S(2)}) collective-permute-start(bf16[2,128,8,128]{3,1,2,0:T(8,128)(2,1)S(1)} %get-tuple-element.428), channel_id=1, source_target_pairs={{2,0},{4,2},{6,4},{8,6},{10,8},{12,10},{14,12},{16,14},{18,16},{20... | collective-permute-start | bytes 1572872 | tf_op jit(solution)/shard_map/while/body/eval_jaxpr/ppermute | solution.py:16
  582.6 26.6 %collective-permute-start.1 = (bf16[2,128,8,128]{3,1,2,0:T(8,128)(2,1)S(1)}, bf16[2,128,8,128]{3,1,2,0:T(8,128)(2,1)S(1)}, u32[]{:S(2)}, u32[]{:S(2)}) collective-permute-start(bf16[2,128,8,128]{3,1,2,0:T(8,128)(2,1)S(1)} %get-tuple-element.428), channel_id=1, source_target_pairs={{2,0},{4,2},{6,4},{8,6},{10,8},{12,10},{14,12},{16,14},{18,16},{20... | collective-permute-start | bytes 1572872 | tf_op jit(solution)/shard_map/while/body/eval_jaxpr/ppermute | solution.py:16
  611.0 28.4 %collective-permute-start.1 = (bf16[2,128,8,128]{3,1,2,0:T(8,128)(2,1)S(1)}, bf16[2,128,8,128]{3,1,2,0:T(8,128)(2,1)S(1)}, u32[]{:S(2)}, u32[]{:S(2)}) collective-permute-start(bf16[2,128,8,128]{3,1,2,0:T(8,128)(2,1)S(1)} %get-tuple-element.428), channel_id=1, source_target_pairs={{2,0},{4,2},{6,4},{8,6},{10,8},{12,10},{14,12},{16,14},{18,16},{20... | collective-permute-start | bytes 1572872 | tf_op jit(solution)/shard_map/while/body/eval_jaxpr/ppermute | solution.py:16
  641.3 26.6 %collective-permute-start.1 = (bf16[2,128,8,128]{3,1,2,0:T(8,128)(2,1)S(1)}, bf16[2,128,8,128]{3,1,2,0:T(8,128)(2,1)S(1)}, u32[]{:S(2)}, u32[]{:S(2)}) collective-permute-start(bf16[2,128,8,128]{3,1,2,0:T(8,128)(2,1)S(1)} %get-tuple-element.428), channel_id=1, source_target_pairs={{2,0},{4,2},{6,4},{8,6},{10,8},{12,10},{14,12},{16,14},{18,16},{20... | collective-permute-start | bytes 1572872 | tf_op jit(solution)/shard_map/while/body/eval_jaxpr/ppermute | solution.py:16
  669.8 28.4 %collective-permute-start.1 = (bf16[2,128,8,128]{3,1,2,0:T(8,128)(2,1)S(1)}, bf16[2,128,8,128]{3,1,2,0:T(8,128)(2,1)S(1)}, u32[]{:S(2)}, u32[]{:S(2)}) collective-permute-start(bf16[2,128,8,128]{3,1,2,0:T(8,128)(2,1)S(1)} %get-tuple-element.428), channel_id=1, source_target_pairs={{2,0},{4,2},{6,4},{8,6},{10,8},{12,10},{14,12},{16,14},{18,16},{20... | collective-permute-start | bytes 1572872 | tf_op jit(solution)/shard_map/while/body/eval_jaxpr/ppermute | solution.py:16
  700.1 26.6 %collective-permute-start.1 = (bf16[2,128,8,128]{3,1,2,0:T(8,128)(2,1)S(1)}, bf16[2,128,8,128]{3,1,2,0:T(8,128)(2,1)S(1)}, u32[]{:S(2)}, u32[]{:S(2)}) collective-permute-start(bf16[2,128,8,128]{3,1,2,0:T(8,128)(2,1)S(1)} %get-tuple-element.428), channel_id=1, source_target_pairs={{2,0},{4,2},{6,4},{8,6},{10,8},{12,10},{14,12},{16,14},{18,16},{20... | collective-permute-start | bytes 1572872 | tf_op jit(solution)/shard_map/while/body/eval_jaxpr/ppermute | solution.py:16
  728.5 28.4 %collective-permute-start.1 = (bf16[2,128,8,128]{3,1,2,0:T(8,128)(2,1)S(1)}, bf16[2,128,8,128]{3,1,2,0:T(8,128)(2,1)S(1)}, u32[]{:S(2)}, u32[]{:S(2)}) collective-permute-start(bf16[2,128,8,128]{3,1,2,0:T(8,128)(2,1)S(1)} %get-tuple-element.428), channel_id=1, source_target_pairs={{2,0},{4,2},{6,4},{8,6},{10,8},{12,10},{14,12},{16,14},{18,16},{20... | collective-permute-start | bytes 1572872 | tf_op jit(solution)/shard_map/while/body/eval_jaxpr/ppermute | solution.py:16
  758.8 26.6 %collective-permute-start.1 = (bf16[2,128,8,128]{3,1,2,0:T(8,128)(2,1)S(1)}, bf16[2,128,8,128]{3,1,2,0:T(8,128)(2,1)S(1)}, u32[]{:S(2)}, u32[]{:S(2)}) collective-permute-start(bf16[2,128,8,128]{3,1,2,0:T(8,128)(2,1)S(1)} %get-tuple-element.428), channel_id=1, source_target_pairs={{2,0},{4,2},{6,4},{8,6},{10,8},{12,10},{14,12},{16,14},{18,16},{20... | collective-permute-start | bytes 1572872 | tf_op jit(solution)/shard_map/while/body/eval_jaxpr/ppermute | solution.py:16
  791.5 170.5 %reduce-scatter.2.cloned.1.call-start = ((), (), s32[]{:S(2)}) async-start(), calls=%async_computation.7 | async-start | bytes 7077888 | tf_op jit(solution)/shard_map/reduce_scatter | solution.py:227
  962.0 85.6 %all-to-all-start.2 = ((bf16[16,72,1024]{2,1,0:T(8,128)(2,1)}), bf16[16,72,1024]{2,1,0:T(8,128)(2,1)S(1)}, u32[]{:S(2)}, u32[]{:S(2)}) async-start(bf16[16,72,1024]{2,1,0:T(8,128)(2,1)} %bitcast.102), calls=%async_computation.3 | async-start | bytes 4718592 | tf_op jit(solution)/shard_map/all_to_all | solution.py:230
  (26 other events, 695.1 us)
Sparse Core Ops, SparseCore 0:
  10.9 272.9 all-gather.2
  286.6 137.9 all-gather.4
  791.6 20.3 all-reduce.1
  949.1 12.8 reduce-scatter.1
where the time goes:
time: 1070 us; the launch traced here: 1060 us
  waiting for transfers between devices  612 us (57%)
  blocking collectives  188 us (18%)
  starting transfers between devices  123 us (11%)
  matrix products  48.1 us (4%)
  other arithmetic  45.3 us (4%)
  local copies, waits for them, and re-layouts  31.9 us (3%)
  between operations  13.6 us (1%)
    ppermute x32, waiting for transfers between devices, from_behind(): lax.ppermute(value, axis, [(source, source + steps) for source in range(f...  349 us
    all_gather x1, waiting for transfers between devices, shards(): stack_piece = lax.all_gather(stack_local, 'seq', axis=0, tiled=True)  234 us
    all_to_all x1, blocking collectives, shards(): lax.all_to_all(buffer, 'seq', split_axis=0, concat_axis=0, tiled=True)  110 us
    ppermute x32, starting transfers between devices, from_behind(): lax.ppermute(value, axis, [(source, source + steps) for source in range(f...  108 us
    all_gather x1, blocking collectives, shards(): router_piece = lax.all_gather(router_local, 'seq', axis=0, tiled=True)  78.2 us
  transfers between devices with their start and end apart: 38, of which 19 were waited for; matrix products, arithmetic and copies ran while one was open for 9% of the time, Pallas kernels for 0%

commit v1 on v0

--- a/solution.py
+++ b/solution.py
@@ -119,7 +119,12 @@
     stack_local = jnp.concatenate([w_query, w_key, w_value], axis=1).astype(jnp.bfloat16)
     router_local = router.astype(jnp.bfloat16)
     stack_piece = lax.all_gather(stack_local, "seq", axis=0, tiled=True)
-    router_piece = lax.all_gather(router_local, "seq", axis=0, tiled=True)
+    ring = [router_local]
+    for hop in range(15):
+        ring.append(lax.ppermute(ring[-1], "seq", [(dev, (dev + 1) % 16) for dev in range(16)]))
+    router_piece = jnp.roll(
+        jnp.concatenate(ring[::-1], axis=0), (lax.axis_index("seq") + 1) * ring[0].shape[0], axis=0
+    )
     product = jnp.dot(normed, stack_piece, preferred_element_type=jnp.float32)
     router_full = router_piece
     product, router_full = (product, router_full)

time: 1070 us -> 1110 us (1.037)
  waiting for transfers between devices: 612 us -> 695 us
  blocking collectives: 188 us -> 110 us
  starting transfers between devices: 123 us -> 164 us
    all_gather x1 -> x0, blocking collectives: 78.2 us -> none  [shards(): router_piece = lax.all_gather(router_local, 'seq', axis=0, tiled=True)]
    ppermute x0 -> x15, waiting for transfers between devices: none -> 63.3 us  [shards(): lax.ppermute(ring[-1], 'seq', [(dev, (dev + 1) % 16) for dev in range(16)])]
    all_to_all x1, waiting for transfers between devices: 0.01 us -> 32.9 us  [shards(): lax.all_to_all(summed.reshape(seq_count * local_experts, item_count, col_...]
    all_to_all x1, starting transfers between devices: 6.97 us -> 34.7 us  [shards(): lax.all_to_all(summed.reshape(seq_count * local_experts, item_count, col_...]
    ppermute x0 -> x15, starting transfers between devices: none -> 13.1 us  [shards(): lax.ppermute(ring[-1], 'seq', [(dev, (dev + 1) % 16) for dev in range(16)])]
    reduce_scatter x1, waiting for transfers between devices: 13 us -> 0.01 us  [shards(): lax.psum_scatter(partial_rows.astype(jnp.bfloat16), 'tp', scatter_dimensi...]
  transfers between devices with their start and end apart: 38 -> 53, of which waited for: 19 -> 33; matrix products, arithmetic and copies ran while one was open for 9% -> 8% of each run, Pallas kernels for 0% -> 0%
where the time goes in v1:
time: 1110 us
  waiting for transfers between devices  695 us (63%)
  starting transfers between devices  164 us (15%)
  blocking collectives  110 us (10%)
  matrix products  48.1 us (4%)
  other arithmetic  45.3 us (4%)
  local copies, waits for them, and re-layouts  32.8 us (3%)
  between operations  13.7 us (1%)
    ppermute x32, waiting for transfers between devices, from_behind(): lax.ppermute(value, axis, [(source, source + steps) for source in range(f...  349 us
    all_gather x1, waiting for transfers between devices, shards(): stack_piece = lax.all_gather(stack_local, 'seq', axis=0, tiled=True)  234 us
    all_to_all x1, blocking collectives, shards(): lax.all_to_all(buffer, 'seq', split_axis=0, concat_axis=0, tiled=True)  110 us
    ppermute x32, starting transfers between devices, from_behind(): lax.ppermute(value, axis, [(source, source + steps) for source in range(f...  108 us
    ppermute x15, waiting for transfers between devices, shards(): lax.ppermute(ring[-1], 'seq', [(dev, (dev + 1) % 16) for dev in range(16)])  63.3 us
    all_to_all x1, starting transfers between devices, shards(): lax.all_to_all(summed.reshape(seq_count * local_experts, item_count, col_...  34.7 us
    all_to_all x1, waiting for transfers between devices, shards(): lax.all_to_all(summed.reshape(seq_count * local_experts, item_count, col_...  32.9 us
  transfers between devices with their start and end apart: 53, of which 33 were waited for; matrix products, arithmetic and copies ran while one was open for 8% of the time, Pallas kernels for 0%

profile of v1, /device:TPU:18, one launch (start us, length us, event | category | flops | bytes accessed | tf_op | source)
XLA Modules:
  0.0 1111.2 jit_solution(5125734608248558720)
XLA Ops:
  35.2 7.2 all-to-all-start
  50.4 233.6 %all-gather.3.cloned.1.call-done = bf16[2048,3072]{1,0:T(8,128)(2,1)} async-done(((bf16[128,3072]{1,0:T(8,128)(2,1)}), bf16[2048,3072]{1,0:T(8,128)(2,1)}) %all-gather.3.cloned.1.call-update) | async-done | bytes 12582928 | tf_op jit(solution)/shard_map/all_gather | solution.py:121
  293.5 493.9 %while.25 = (s32[]{:T(128)}, f32[8,128]{1,0:T(8,128)S(1)}, f32[8,128]{1,0:T(8,128)S(1)}, f32[8,128,128]{2,1,0:T(8,128)S(1)}, bf16[2,128,8,128]{3,1,2,0:T(8,128)(...) while((s32[]{:T(128)}, f32[8,128]{1,0:T(8,128)S(1)}, ...), condition=%wide.region_8.9_spmd.clone, body=%wide.region_4.8_spmd.clone.sunk | while | flops 471806848 | bytes 14038749 | solution.py:167
  300.6 23.3 %collective-permute-done = bf16[2,128,8,128]{3,1,2,0:T(8,128)(2,1)S(1)} collective-permute-done((bf16[2,128,8,128]{3,1,2,0:T(8,128)(2,1)S(1)}, bf16[2,128,8,128]{3,1,2,0:T(8,128)(2,1)S(1)}, u32[]{:S(2)}, u32[]{:S(2)}) %collective-permute-start) | collective-permute-done | bytes 524320 | tf_op jit(solution)/shard_map/while/body/eval_jaxpr/ppermute | solution.py:16
  332.9 20.7 %collective-permute-done = bf16[2,128,8,128]{3,1,2,0:T(8,128)(2,1)S(1)} collective-permute-done((bf16[2,128,8,128]{3,1,2,0:T(8,128)(2,1)S(1)}, bf16[2,128,8,128]{3,1,2,0:T(8,128)(2,1)S(1)}, u32[]{:S(2)}, u32[]{:S(2)}) %collective-permute-start) | collective-permute-done | bytes 524320 | tf_op jit(solution)/shard_map/while/body/eval_jaxpr/ppermute | solution.py:16
  362.6 41.3 %collective-permute-done = bf16[2,128,8,128]{3,1,2,0:T(8,128)(2,1)S(1)} collective-permute-done((bf16[2,128,8,128]{3,1,2,0:T(8,128)(2,1)S(1)}, bf16[2,128,8,128]{3,1,2,0:T(8,128)(2,1)S(1)}, u32[]{:S(2)}, u32[]{:S(2)}) %collective-permute-start) | collective-permute-done | bytes 524320 | tf_op jit(solution)/shard_map/while/body/eval_jaxpr/ppermute | solution.py:16
  413.4 21.1 %collective-permute-done = bf16[2,128,8,128]{3,1,2,0:T(8,128)(2,1)S(1)} collective-permute-done((bf16[2,128,8,128]{3,1,2,0:T(8,128)(2,1)S(1)}, bf16[2,128,8,128]{3,1,2,0:T(8,128)(2,1)S(1)}, u32[]{:S(2)}, u32[]{:S(2)}) %collective-permute-start) | collective-permute-done | bytes 524320 | tf_op jit(solution)/shard_map/while/body/eval_jaxpr/ppermute | solution.py:16
  443.5 19.7 %collective-permute-done = bf16[2,128,8,128]{3,1,2,0:T(8,128)(2,1)S(1)} collective-permute-done((bf16[2,128,8,128]{3,1,2,0:T(8,128)(2,1)S(1)}, bf16[2,128,8,128]{3,1,2,0:T(8,128)(2,1)S(1)}, u32[]{:S(2)}, u32[]{:S(2)}) %collective-permute-start) | collective-permute-done | bytes 524320 | tf_op jit(solution)/shard_map/while/body/eval_jaxpr/ppermute | solution.py:16
  472.3 19.5 %collective-permute-done = bf16[2,128,8,128]{3,1,2,0:T(8,128)(2,1)S(1)} collective-permute-done((bf16[2,128,8,128]{3,1,2,0:T(8,128)(2,1)S(1)}, bf16[2,128,8,128]{3,1,2,0:T(8,128)(2,1)S(1)}, u32[]{:S(2)}, u32[]{:S(2)}) %collective-permute-start) | collective-permute-done | bytes 524320 | tf_op jit(solution)/shard_map/while/body/eval_jaxpr/ppermute | solution.py:16
  500.7 21.3 %collective-permute-done = bf16[2,128,8,128]{3,1,2,0:T(8,128)(2,1)S(1)} collective-permute-done((bf16[2,128,8,128]{3,1,2,0:T(8,128)(2,1)S(1)}, bf16[2,128,8,128]{3,1,2,0:T(8,128)(2,1)S(1)}, u32[]{:S(2)}, u32[]{:S(2)}) %collective-permute-start) | collective-permute-done | bytes 524320 | tf_op jit(solution)/shard_map/while/body/eval_jaxpr/ppermute | solution.py:16
  531.0 19.5 %collective-permute-done = bf16[2,128,8,128]{3,1,2,0:T(8,128)(2,1)S(1)} collective-permute-done((bf16[2,128,8,128]{3,1,2,0:T(8,128)(2,1)S(1)}, bf16[2,128,8,128]{3,1,2,0:T(8,128)(2,1)S(1)}, u32[]{:S(2)}, u32[]{:S(2)}) %collective-permute-start) | collective-permute-done | bytes 524320 | tf_op jit(solution)/shard_map/while/body/eval_jaxpr/ppermute | solution.py:16
  559.5 21.3 %collective-permute-done = bf16[2,128,8,128]{3,1,2,0:T(8,128)(2,1)S(1)} collective-permute-done((bf16[2,128,8,128]{3,1,2,0:T(8,128)(2,1)S(1)}, bf16[2,128,8,128]{3,1,2,0:T(8,128)(2,1)S(1)}, u32[]{:S(2)}, u32[]{:S(2)}) %collective-permute-start) | collective-permute-done | bytes 524320 | tf_op jit(solution)/shard_map/while/body/eval_jaxpr/ppermute | solution.py:16
  589.7 19.5 %collective-permute-done = bf16[2,128,8,128]{3,1,2,0:T(8,128)(2,1)S(1)} collective-permute-done((bf16[2,128,8,128]{3,1,2,0:T(8,128)(2,1)S(1)}, bf16[2,128,8,128]{3,1,2,0:T(8,128)(2,1)S(1)}, u32[]{:S(2)}, u32[]{:S(2)}) %collective-permute-start) | collective-permute-done | bytes 524320 | tf_op jit(solution)/shard_map/while/body/eval_jaxpr/ppermute | solution.py:16
  618.2 21.3 %collective-permute-done = bf16[2,128,8,128]{3,1,2,0:T(8,128)(2,1)S(1)} collective-permute-done((bf16[2,128,8,128]{3,1,2,0:T(8,128)(2,1)S(1)}, bf16[2,128,8,128]{3,1,2,0:T(8,128)(2,1)S(1)}, u32[]{:S(2)}, u32[]{:S(2)}) %collective-permute-start) | collective-permute-done | bytes 524320 | tf_op jit(solution)/shard_map/while/body/eval_jaxpr/ppermute | solution.py:16
  648.5 19.5 %collective-permute-done = bf16[2,128,8,128]{3,1,2,0:T(8,128)(2,1)S(1)} collective-permute-done((bf16[2,128,8,128]{3,1,2,0:T(8,128)(2,1)S(1)}, bf16[2,128,8,128]{3,1,2,0:T(8,128)(2,1)S(1)}, u32[]{:S(2)}, u32[]{:S(2)}) %collective-permute-start) | collective-permute-done | bytes 524320 | tf_op jit(solution)/shard_map/while/body/eval_jaxpr/ppermute | solution.py:16
  676.9 21.3 %collective-permute-done = bf16[2,128,8,128]{3,1,2,0:T(8,128)(2,1)S(1)} collective-permute-done((bf16[2,128,8,128]{3,1,2,0:T(8,128)(2,1)S(1)}, bf16[2,128,8,128]{3,1,2,0:T(8,128)(2,1)S(1)}, u32[]{:S(2)}, u32[]{:S(2)}) %collective-permute-start) | collective-permute-done | bytes 524320 | tf_op jit(solution)/shard_map/while/body/eval_jaxpr/ppermute | solution.py:16
  707.2 19.5 %collective-permute-done = bf16[2,128,8,128]{3,1,2,0:T(8,128)(2,1)S(1)} collective-permute-done((bf16[2,128,8,128]{3,1,2,0:T(8,128)(2,1)S(1)}, bf16[2,128,8,128]{3,1,2,0:T(8,128)(2,1)S(1)}, u32[]{:S(2)}, u32[]{:S(2)}) %collective-permute-start) | collective-permute-done | bytes 524320 | tf_op jit(solution)/shard_map/while/body/eval_jaxpr/ppermute | solution.py:16
  735.7 21.3 %collective-permute-done = bf16[2,128,8,128]{3,1,2,0:T(8,128)(2,1)S(1)} collective-permute-done((bf16[2,128,8,128]{3,1,2,0:T(8,128)(2,1)S(1)}, bf16[2,128,8,128]{3,1,2,0:T(8,128)(2,1)S(1)}, u32[]{:S(2)}, u32[]{:S(2)}) %collective-permute-start) | collective-permute-done | bytes 524320 | tf_op jit(solution)/shard_map/while/body/eval_jaxpr/ppermute | solution.py:16
  765.9 19.5 %collective-permute-done = bf16[2,128,8,128]{3,1,2,0:T(8,128)(2,1)S(1)} collective-permute-done((bf16[2,128,8,128]{3,1,2,0:T(8,128)(2,1)S(1)}, bf16[2,128,8,128]{3,1,2,0:T(8,128)(2,1)S(1)}, u32[]{:S(2)}, u32[]{:S(2)}) %collective-permute-start) | collective-permute-done | bytes 524320 | tf_op jit(solution)/shard_map/while/body/eval_jaxpr/ppermute | solution.py:16
  796.2 15.8 %all-reduce.2.cloned.1.call-done = f32[128,2048]{1,0:T(8,128)} async-done(((f32[128,2048]{1,0:T(8,128)}), f32[128,2048]{1,0:T(8,128)}) %all-reduce.2.cloned.1.call-update) | async-done | bytes 1048592 | tf_op jit(solution)/shard_map/psum | solution.py:181
  825.4 110.3 %all_to_all.22 = bf16[16,72,2048]{2,1,0:T(8,128)(2,1)S(1)} all-to-all(bf16[16,72,2048]{2,1,0:T(8,128)(2,1)} %broadcast_select_fusion.1), channel_id=1, replica_groups=mesh['seq'=16,'tp'=2] {'seq'}, dimensions={0} | all-to-all | bytes 9437184 | tf_op jit(solution)/shard_map/all_to_all | solution.py:213
  935.7 7.3 fusion.14
  1026.1 34.7 %all-to-all-start.2 = ((bf16[16,72,1024]{2,1,0:T(8,128)(2,1)}), bf16[16,72,1024]{2,1,0:T(8,128)(2,1)S(1)}, u32[]{:S(2)}, u32[]{:S(2)}) async-start(bf16[16,72,1024]{2,1,0:T(8,128)(2,1)} %bitcast.101), calls=%async_computation.3 | async-start | bytes 4718592 | tf_op jit(solution)/shard_map/all_to_all | solution.py:235
  1061.7 32.9 %all-to-all-done.2 = bf16[16,72,1024]{2,1,0:T(8,128)(2,1)S(1)} async-done(((bf16[16,72,1024]{2,1,0:T(8,128)(2,1)}), bf16[16,72,1024]{2,1,0:T(8,128)(2,1)S(1)}, u32[]{:S(2)}, u32[]{:S(2)}) %all-to-all-start.2) | async-done | bytes 2359328 | tf_op jit(solution)/shard_map/all_to_all | solution.py:235
  (492 shorter events, 304.1 us)
Async XLA Ops:
  6.5 277.5 %all-gather.3.cloned.1.call-start = ((), (), s32[]{:S(2)}) async-start(), calls=%async_computation.4 | async-start | bytes 13369344 | tf_op jit(solution)/shard_map/all_gather | solution.py:121
  35.2 790.2 %all-to-all-start = ((bf16[16,128,1536]{2,1,0:T(8,128)(2,1)}), bf16[16,128,1536]{2,1,0:T(8,128)(2,1)}, u32[]{:S(2)}, u32[]{:S(2)}) async-start(bf16[16,128,1536]{2,1,0:T(8,128)(2,1)} %broadcast_select_fusion), calls=%async_computation | async-start | bytes 12582912 | tf_op jit(solution)/shard_map/all_to_all | solution.py:210
  42.5 745.1 %all-gather.5.cloned.1.call-start = ((), (), s32[]{:S(2)}) async-start(), calls=%async_computation.5 | async-start | bytes 4456448 | tf_op jit(solution)/shard_map/all_gather | solution.py:178
  43.3 768.7 %all-reduce.2.cloned.1.call-start = ((), (), s32[]{:S(2)}) async-start(), calls=%async_computation.6 | async-start | bytes 2097152 | tf_op jit(solution)/shard_map/psum | solution.py:181
  293.5 30.4 %collective-permute-start.1 = (bf16[2,128,8,128]{3,1,2,0:T(8,128)(2,1)S(1)}, bf16[2,128,8,128]{3,1,2,0:T(8,128)(2,1)S(1)}, u32[]{:S(2)}, u32[]{:S(2)}) collective-permute-start(bf16[2,128,8,128]{3,1,2,0:T(8,128)(2,1)S(1)} %get-tuple-element.428), channel_id=1, source_target_pairs={{2,0},{4,2},{6,4},{8,6},{10,8},{12,10},{14,12},{16,14},{18,16},{20... | collective-permute-start | bytes 1572872 | tf_op jit(solution)/shard_map/while/body/eval_jaxpr/ppermute | solution.py:16
  296.2 27.7 %collective-permute-start = (bf16[2,128,8,128]{3,1,2,0:T(8,128)(2,1)S(1)}, bf16[2,128,8,128]{3,1,2,0:T(8,128)(2,1)S(1)}, u32[]{:S(2)}, u32[]{:S(2)}) collective-permute-start(bf16[2,128,8,128]{3,1,2,0:T(8,128)(2,1)S(1)} %get-tuple-element.427), channel_id=1, source_target_pairs={{0,2},{2,4},{4,6},{6,8},{8,10},{10,12},{12,14},{14,16},{16,18},{18... | collective-permute-start | bytes 1572872 | tf_op jit(solution)/shard_map/while/body/eval_jaxpr/ppermute | solution.py:16
  325.8 27.9 %collective-permute-start.1 = (bf16[2,128,8,128]{3,1,2,0:T(8,128)(2,1)S(1)}, bf16[2,128,8,128]{3,1,2,0:T(8,128)(2,1)S(1)}, u32[]{:S(2)}, u32[]{:S(2)}) collective-permute-start(bf16[2,128,8,128]{3,1,2,0:T(8,128)(2,1)S(1)} %get-tuple-element.428), channel_id=1, source_target_pairs={{2,0},{4,2},{6,4},{8,6},{10,8},{12,10},{14,12},{16,14},{18,16},{20... | collective-permute-start | bytes 1572872 | tf_op jit(solution)/shard_map/while/body/eval_jaxpr/ppermute | solution.py:16
  355.5 48.5 %collective-permute-start.1 = (bf16[2,128,8,128]{3,1,2,0:T(8,128)(2,1)S(1)}, bf16[2,128,8,128]{3,1,2,0:T(8,128)(2,1)S(1)}, u32[]{:S(2)}, u32[]{:S(2)}) collective-permute-start(bf16[2,128,8,128]{3,1,2,0:T(8,128)(2,1)S(1)} %get-tuple-element.428), channel_id=1, source_target_pairs={{2,0},{4,2},{6,4},{8,6},{10,8},{12,10},{14,12},{16,14},{18,16},{20... | collective-permute-start | bytes 1572872 | tf_op jit(solution)/shard_map/while/body/eval_jaxpr/ppermute | solution.py:16
  359.3 44.6 %collective-permute-start = (bf16[2,128,8,128]{3,1,2,0:T(8,128)(2,1)S(1)}, bf16[2,128,8,128]{3,1,2,0:T(8,128)(2,1)S(1)}, u32[]{:S(2)}, u32[]{:S(2)}) collective-permute-start(bf16[2,128,8,128]{3,1,2,0:T(8,128)(2,1)S(1)} %get-tuple-element.427), channel_id=1, source_target_pairs={{0,2},{2,4},{4,6},{6,8},{8,10},{10,12},{12,14},{14,16},{16,18},{18... | collective-permute-start | bytes 1572872 | tf_op jit(solution)/shard_map/while/body/eval_jaxpr/ppermute | solution.py:16
  405.8 28.8 %collective-permute-start.1 = (bf16[2,128,8,128]{3,1,2,0:T(8,128)(2,1)S(1)}, bf16[2,128,8,128]{3,1,2,0:T(8,128)(2,1)S(1)}, u32[]{:S(2)}, u32[]{:S(2)}) collective-permute-start(bf16[2,128,8,128]{3,1,2,0:T(8,128)(2,1)S(1)} %get-tuple-element.428), channel_id=1, source_target_pairs={{2,0},{4,2},{6,4},{8,6},{10,8},{12,10},{14,12},{16,14},{18,16},{20... | collective-permute-start | bytes 1572872 | tf_op jit(solution)/shard_map/while/body/eval_jaxpr/ppermute | solution.py:16
  407.7 26.8 %collective-permute-start = (bf16[2,128,8,128]{3,1,2,0:T(8,128)(2,1)S(1)}, bf16[2,128,8,128]{3,1,2,0:T(8,128)(2,1)S(1)}, u32[]{:S(2)}, u32[]{:S(2)}) collective-permute-start(bf16[2,128,8,128]{3,1,2,0:T(8,128)(2,1)S(1)} %get-tuple-element.427), channel_id=1, source_target_pairs={{0,2},{2,4},{4,6},{6,8},{8,10},{10,12},{12,14},{14,16},{16,18},{18... | collective-permute-start | bytes 1572872 | tf_op jit(solution)/shard_map/while/body/eval_jaxpr/ppermute | solution.py:16
  436.4 26.9 %collective-permute-start.1 = (bf16[2,128,8,128]{3,1,2,0:T(8,128)(2,1)S(1)}, bf16[2,128,8,128]{3,1,2,0:T(8,128)(2,1)S(1)}, u32[]{:S(2)}, u32[]{:S(2)}) collective-permute-start(bf16[2,128,8,128]{3,1,2,0:T(8,128)(2,1)S(1)} %get-tuple-element.428), channel_id=1, source_target_pairs={{2,0},{4,2},{6,4},{8,6},{10,8},{12,10},{14,12},{16,14},{18,16},{20... | collective-permute-start | bytes 1572872 | tf_op jit(solution)/shard_map/while/body/eval_jaxpr/ppermute | solution.py:16
  493.6 28.4 %collective-permute-start.1 = (bf16[2,128,8,128]{3,1,2,0:T(8,128)(2,1)S(1)}, bf16[2,128,8,128]{3,1,2,0:T(8,128)(2,1)S(1)}, u32[]{:S(2)}, u32[]{:S(2)}) collective-permute-start(bf16[2,128,8,128]{3,1,2,0:T(8,128)(2,1)S(1)} %get-tuple-element.428), channel_id=1, source_target_pairs={{2,0},{4,2},{6,4},{8,6},{10,8},{12,10},{14,12},{16,14},{18,16},{20... | collective-permute-start | bytes 1572872 | tf_op jit(solution)/shard_map/while/body/eval_jaxpr/ppermute | solution.py:16
  552.4 28.4 %collective-permute-start.1 = (bf16[2,128,8,128]{3,1,2,0:T(8,128)(2,1)S(1)}, bf16[2,128,8,128]{3,1,2,0:T(8,128)(2,1)S(1)}, u32[]{:S(2)}, u32[]{:S(2)}) collective-permute-start(bf16[2,128,8,128]{3,1,2,0:T(8,128)(2,1)S(1)} %get-tuple-element.428), channel_id=1, source_target_pairs={{2,0},{4,2},{6,4},{8,6},{10,8},{12,10},{14,12},{16,14},{18,16},{20... | collective-permute-start | bytes 1572872 | tf_op jit(solution)/shard_map/while/body/eval_jaxpr/ppermute | solution.py:16
  582.6 26.6 %collective-permute-start.1 = (bf16[2,128,8,128]{3,1,2,0:T(8,128)(2,1)S(1)}, bf16[2,128,8,128]{3,1,2,0:T(8,128)(2,1)S(1)}, u32[]{:S(2)}, u32[]{:S(2)}) collective-permute-start(bf16[2,128,8,128]{3,1,2,0:T(8,128)(2,1)S(1)} %get-tuple-element.428), channel_id=1, source_target_pairs={{2,0},{4,2},{6,4},{8,6},{10,8},{12,10},{14,12},{16,14},{18,16},{20... | collective-permute-start | bytes 1572872 | tf_op jit(solution)/shard_map/while/body/eval_jaxpr/ppermute | solution.py:16
  611.1 28.4 %collective-permute-start.1 = (bf16[2,128,8,128]{3,1,2,0:T(8,128)(2,1)S(1)}, bf16[2,128,8,128]{3,1,2,0:T(8,128)(2,1)S(1)}, u32[]{:S(2)}, u32[]{:S(2)}) collective-permute-start(bf16[2,128,8,128]{3,1,2,0:T(8,128)(2,1)S(1)} %get-tuple-element.428), channel_id=1, source_target_pairs={{2,0},{4,2},{6,4},{8,6},{10,8},{12,10},{14,12},{16,14},{18,16},{20... | collective-permute-start | bytes 1572872 | tf_op jit(solution)/shard_map/while/body/eval_jaxpr/ppermute | solution.py:16
  641.4 26.6 %collective-permute-start.1 = (bf16[2,128,8,128]{3,1,2,0:T(8,128)(2,1)S(1)}, bf16[2,128,8,128]{3,1,2,0:T(8,128)(2,1)S(1)}, u32[]{:S(2)}, u32[]{:S(2)}) collective-permute-start(bf16[2,128,8,128]{3,1,2,0:T(8,128)(2,1)S(1)} %get-tuple-element.428), channel_id=1, source_target_pairs={{2,0},{4,2},{6,4},{8,6},{10,8},{12,10},{14,12},{16,14},{18,16},{20... | collective-permute-start | bytes 1572872 | tf_op jit(solution)/shard_map/while/body/eval_jaxpr/ppermute | solution.py:16
  669.9 28.4 %collective-permute-start.1 = (bf16[2,128,8,128]{3,1,2,0:T(8,128)(2,1)S(1)}, bf16[2,128,8,128]{3,1,2,0:T(8,128)(2,1)S(1)}, u32[]{:S(2)}, u32[]{:S(2)}) collective-permute-start(bf16[2,128,8,128]{3,1,2,0:T(8,128)(2,1)S(1)} %get-tuple-element.428), channel_id=1, source_target_pairs={{2,0},{4,2},{6,4},{8,6},{10,8},{12,10},{14,12},{16,14},{18,16},{20... | collective-permute-start | bytes 1572872 | tf_op jit(solution)/shard_map/while/body/eval_jaxpr/ppermute | solution.py:16
  700.1 26.6 %collective-permute-start.1 = (bf16[2,128,8,128]{3,1,2,0:T(8,128)(2,1)S(1)}, bf16[2,128,8,128]{3,1,2,0:T(8,128)(2,1)S(1)}, u32[]{:S(2)}, u32[]{:S(2)}) collective-permute-start(bf16[2,128,8,128]{3,1,2,0:T(8,128)(2,1)S(1)} %get-tuple-element.428), channel_id=1, source_target_pairs={{2,0},{4,2},{6,4},{8,6},{10,8},{12,10},{14,12},{16,14},{18,16},{20... | collective-permute-start | bytes 1572872 | tf_op jit(solution)/shard_map/while/body/eval_jaxpr/ppermute | solution.py:16
  728.6 28.4 %collective-permute-start.1 = (bf16[2,128,8,128]{3,1,2,0:T(8,128)(2,1)S(1)}, bf16[2,128,8,128]{3,1,2,0:T(8,128)(2,1)S(1)}, u32[]{:S(2)}, u32[]{:S(2)}) collective-permute-start(bf16[2,128,8,128]{3,1,2,0:T(8,128)(2,1)S(1)} %get-tuple-element.428), channel_id=1, source_target_pairs={{2,0},{4,2},{6,4},{8,6},{10,8},{12,10},{14,12},{16,14},{18,16},{20... | collective-permute-start | bytes 1572872 | tf_op jit(solution)/shard_map/while/body/eval_jaxpr/ppermute | solution.py:16
  758.8 26.6 %collective-permute-start.1 = (bf16[2,128,8,128]{3,1,2,0:T(8,128)(2,1)S(1)}, bf16[2,128,8,128]{3,1,2,0:T(8,128)(2,1)S(1)}, u32[]{:S(2)}, u32[]{:S(2)}) collective-permute-start(bf16[2,128,8,128]{3,1,2,0:T(8,128)(2,1)S(1)} %get-tuple-element.428), channel_id=1, source_target_pairs={{2,0},{4,2},{6,4},{8,6},{10,8},{12,10},{14,12},{16,14},{18,16},{20... | collective-permute-start | bytes 1572872 | tf_op jit(solution)/shard_map/while/body/eval_jaxpr/ppermute | solution.py:16
  791.6 234.6 %reduce-scatter.2.cloned.1.call-start = ((), (), s32[]{:S(2)}) async-start(), calls=%async_computation.7 | async-start | bytes 7077888 | tf_op jit(solution)/shard_map/reduce_scatter | solution.py:232
  1022.1 38.8 %collective-permute-start.16 = (bf16[128,16]{0,1:T(8,128)(2,1)S(1)}, bf16[128,16]{0,1:T(8,128)(2,1)S(1)}, u32[]{:S(2)}, u32[]{:S(2)}) collective-permute-start(bf16[128,16]{0,1:T(8,128)(2,1)S(1)} %collective-permute-done.15), channel_id=1, source_target_pairs={{0,2},{2,4},{4,6},{6,8},{8,10},{10,12},{12,14},{14,16},{16,18},{18... | collective-permute-start | bytes 12296 | tf_op jit(solution)/shard_map/ppermute | solution.py:124
  1026.1 68.5 %all-to-all-start.2 = ((bf16[16,72,1024]{2,1,0:T(8,128)(2,1)}), bf16[16,72,1024]{2,1,0:T(8,128)(2,1)S(1)}, u32[]{:S(2)}, u32[]{:S(2)}) async-start(bf16[16,72,1024]{2,1,0:T(8,128)(2,1)} %bitcast.101), calls=%async_computation.3 | async-start | bytes 4718592 | tf_op jit(solution)/shard_map/all_to_all | solution.py:235
  (41 other events, 774.8 us)
Sparse Core Ops, SparseCore 0:
  10.9 273.0 all-gather.2
  286.7 137.9 all-gather.4
  791.7 20.2 all-reduce.1
  949.1 12.8 reduce-scatter.1
